TPU v7x, 256 devices: a whole 4x4x8 slice. The times are simulated.
256 devices in a mesh: cluster: 8 (over z), sub: 32 (over x, y, core).
Axes of the slice: x: 4, y: 4, z: 8, core: 2. Of those that a mesh axis runs over, the one named last changes fastest.
Arguments:
- dual_ops: bfloat16 [8, 32, 2048, 2048], P('cluster', 'sub'), as said below
- corner_coupling: float32 [8, 32, 48, 2048], P('cluster', 'sub'), may hold values from -0.3 to 0.3
- coarse_inverse: float32 [32, 128, 128], P('sub'), as said below
- corner_map: int32 [8, 32, 48], P('cluster', 'sub'), may hold values from 0 to 127, as said below
- interface_tiles: int32 [8, 32, 4], P('cluster', 'sub'), may hold values from 1 to 4, as said below
- gap_terms: float32 [8, 32, 2048, 128], P('cluster', 'sub')
Outputs:
- multipliers: float32 [8, 32, 2048, 128], P('cluster', 'sub')
- residual: float32 [8, 32, 2048, 128], P('cluster', 'sub')
Inputs may be any that keep to these rules, and one draw needn't show every extreme that they name: interface_tiles[c, s, k] counts the tiles that subdomain (c, s) shares with the subdomain at sub distance -2, -1, +1, +2 for k = 0..3, wrapping around 32; the count for distance +d equals that neighbour's count for distance -d; in every c some subdomain has 4 for all four. `corner_map`: the 48 entries of one subdomain are distinct. `dual_ops`: each matrix is symmetric positive definite. `coarse_inverse`: each matrix is symmetric positive definite.
All inputs are finite; a program needn't handle non-finite values.
Results may differ from a plain program's by a relative error of at most 0.009.
Values sent between devices are 32-bit elements; how exact they have to be, the bound alone decides.
No kernel may reach another device: no remote copies, remote signals or barrier semaphores. Data moves between devices by JAX's collectives and lax.ppermute only.
A program may use at most 64 MiB of HBM per device.

v0:
```python
import jax
import jax.numpy as jnp
from jax import lax
from jax.sharding import PartitionSpec as P

TILE = 128
MAXT = 4
NCOARSE = 128
ITERS = 3


def passed_along(block, axis, distance):
    devices = range(lax.axis_size(axis))
    route = [((i - distance) % len(devices), i) for i in devices]
    return lax.ppermute(block, axis, route)


def extract_run(values_in, start_row, row_count):
    run_rows = MAXT * TILE
    run_block = lax.dynamic_slice_in_dim(values_in, start_row, run_rows, 0)
    keep_mask = jnp.arange(run_rows, dtype=jnp.int32)[:, None] < row_count
    return jnp.where(keep_mask, run_block, jnp.zeros_like(run_block))


def insert_run(run_block, start_row, dual_rows):
    padded = jnp.zeros((dual_rows + run_block.shape[0], run_block.shape[1]), run_block.dtype)
    return lax.dynamic_update_slice_in_dim(padded, run_block, start_row, 0)[:dual_rows]


def local(dual_ops, corner_coupling, coarse_inverse, corner_map, interface_tiles, gap_terms):
    highest = lax.Precision.HIGHEST
    operator = dual_ops[0, 0]
    coupling = corner_coupling[0, 0]
    inverse = coarse_inverse[0]
    corners = corner_map[0, 0]
    lengths = interface_tiles[0, 0] * TILE
    run_start = jnp.concatenate([jnp.zeros((1,), jnp.int32), jnp.cumsum(lengths)[:3]])
    dual_rows = operator.shape[0]
    live_mask = jnp.arange(dual_rows, dtype=jnp.int32)[:, None] < jnp.sum(lengths)
    onehot = (corners[:, None] == jnp.arange(NCOARSE, dtype=jnp.int32)[None, :]).astype(jnp.float32)

    def assemble(values_in):
        incoming = [None, None, None, None]
        for run_index, distance in enumerate((-2, -1, 1, 2)):
            outgoing = extract_run(values_in, run_start[3 - run_index], lengths[3 - run_index])
            incoming[run_index] = passed_along(outgoing, "sub", -distance)
        assembled = jnp.where(live_mask, values_in, jnp.zeros_like(values_in))
        for run_index in range(4):
            assembled = assembled + insert_run(incoming[run_index], run_start[run_index], dual_rows)
        return assembled

    residual = assemble(gap_terms[0, 0])
    direction = residual
    multipliers = jnp.zeros_like(residual)
    norm_now = lax.psum(jnp.sum(residual * residual, axis=0), ("cluster", "sub"))
    for iteration in range(ITERS):
        local_part = jnp.dot(
            operator, direction.astype(jnp.bfloat16), preferred_element_type=jnp.float32
        )
        corner_values = jnp.dot(coupling, direction, precision=highest)
        coarse_part = jnp.dot(onehot.T, corner_values, precision=highest)
        coarse_total = lax.psum(coarse_part, "cluster")
        coarse_solution = jnp.dot(inverse, coarse_total, precision=highest)
        corner_back = jnp.dot(onehot, coarse_solution, precision=highest)
        image = assemble(local_part + jnp.dot(coupling.T, corner_back, precision=highest))
        curvature = lax.psum(jnp.sum(direction * image, axis=0), ("cluster", "sub"))
        step_size = norm_now / curvature
        multipliers = multipliers + step_size * direction
        residual = residual - step_size * image
        norm_next = lax.psum(jnp.sum(residual * residual, axis=0), ("cluster", "sub"))
        direction = residual + norm_next / norm_now * direction
        norm_now = norm_next
    return (multipliers[None, None], residual[None, None])


def solution(mesh):
    in_specs = (
        P("cluster", "sub", None, None),
        P("cluster", "sub", None, None),
        P("sub", None, None),
        P("cluster", "sub", None),
        P("cluster", "sub", None),
        P("cluster", "sub", None, None),
    )
    out_specs = (P("cluster", "sub", None, None), P("cluster", "sub", None, None))
    return jax.shard_map(local, mesh=mesh, in_specs=in_specs, out_specs=out_specs, check_vma=False)
```

profile of v0, /device:TPU:1, one launch (start us, length us, event | category | flops | bytes accessed | tf_op | source)
XLA Modules:
  0.0 746.1 jit_solution(15423645180526299071)
XLA Ops:
  7.2 1.3 fusion.62
  14.9 1.2 constant_dynamic-slice_fusion.1
  16.8 1.2 iota_compare_fusion.6
  18.1 2.8 collective-permute-start.1
  22.6 4.8 collective-permute-start.3
  32.6 1.2 broadcast.85.clone.2
  33.8 1.8 dynamic_update_slice.49
  35.6 1.2 broadcast.85.clone.1
  36.9 1.9 dynamic_update_slice.50
  38.8 1.2 broadcast.85.clone
  40.0 1.8 dynamic_update_slice.51
  41.8 2.2 fusion.12
  46.0 70.0 %all-reduce.9.cloned.1.call-done = f32[128,128]{1,0:T(8,128)} async-done(((f32[128,128]{1,0:T(8,128)}), f32[128,128]{1,0:T(8,128)}) %all-reduce.9.cloned.1.call-update) | async-done | bytes 65552 | tf_op jit(solution)/shard_map/psum | solution.py:62
  116.0 1.1 fusion.43
  118.4 6.3 fusion.6
  125.8 6.7 collective-permute-start.5
  132.6 4.1 collective-permute-start.7
  136.7 1.2 broadcast.85.clone.5
  137.9 1.8 dynamic_update_slice.53
  139.7 1.4 collective-permute-done.6
  141.1 1.2 broadcast.85.clone.4
  142.3 1.9 dynamic_update_slice.54
  144.2 1.2 broadcast.85.clone.3
  145.4 1.8 dynamic_update_slice.55
  147.2 2.8 multiply_reduce_fusion.4
  150.0 78.7 %all-reduce.4 = (f32[128]{0:T(128)S(1)}, f32[128]{0:T(128)S(1)}) all-reduce(f32[128]{0:T(128)} %get-tuple-element.5, f32[128]{0:T(128)} %get-tuple-element.4), channel_id=1, replica_groups=mesh['cluster'=8,'sub'=32] {'cluster','sub'}, use_global_device_ids=true, to_apply=%region_3.4 | all-reduce | flops 256 | bytes 2048 | tf_op jit(solution)/shard_map/psum | solution.py:55
  229.6 72.4 %psum.66 = f32[128]{0:T(128)S(1)} all-reduce(f32[128]{0:T(128)S(1)} %multiply_reduce_fusion.3), channel_id=1, replica_groups=mesh['cluster'=8,'sub'=32] {'cluster','sub'}, use_global_device_ids=true, to_apply=%region_8.9 | all-reduce | flops 128 | bytes 1024 | tf_op jit(solution)/shard_map/psum | solution.py:70
  305.5 7.2 fusion.2
  312.7 56.5 %all-reduce.11.cloned.1.call-done = f32[128,128]{1,0:T(8,128)} async-done(((f32[128,128]{1,0:T(8,128)}), f32[128,128]{1,0:T(8,128)}) %all-reduce.11.cloned.1.call-update) | async-done | bytes 65552 | tf_op jit(solution)/shard_map/psum | solution.py:62
  369.3 1.2 fusion.41
  370.6 2.3 convolution_add_fusion.1
  374.1 6.7 collective-permute-start.9
  381.5 3.6 collective-permute-start.11
  385.3 1.2 broadcast.85.clone.8
  386.5 1.9 dynamic_update_slice.57
  388.4 1.2 collective-permute-done.10
  389.6 1.2 broadcast.85.clone.7
  390.8 1.9 dynamic_update_slice.58
  392.7 1.2 broadcast.85.clone.6
  393.9 1.9 dynamic_update_slice.59
  395.8 4.2 multiply_reduce_fusion.2
  400.0 78.7 %psum.68 = f32[128]{0:T(128)} all-reduce(f32[128]{0:T(128)} %get-tuple-element.12), channel_id=1, replica_groups=mesh['cluster'=8,'sub'=32] {'cluster','sub'}, use_global_device_ids=true, to_apply=%region_11.12 | all-reduce | flops 128 | bytes 1024 | tf_op jit(solution)/shard_map/psum | solution.py:66
  479.3 3.0 multiply_reduce_fusion.1
  482.3 72.5 %psum.69 = f32[128]{0:T(128)S(1)} all-reduce(f32[128]{0:T(128)} %get-tuple-element.10), channel_id=1, replica_groups=mesh['cluster'=8,'sub'=32] {'cluster','sub'}, use_global_device_ids=true, to_apply=%region_13.14 | all-reduce | flops 128 | bytes 1024 | tf_op jit(solution)/shard_map/psum | solution.py:70
  555.4 1.4 multiply_add_fusion
  558.7 7.2 fusion
  565.9 56.7 %all-reduce.13.cloned.1.call-done = f32[128,128]{1,0:T(8,128)} async-done(((f32[128,128]{1,0:T(8,128)}), f32[128,128]{1,0:T(8,128)}) %all-reduce.13.cloned.1.call-update) | async-done | bytes 65552 | tf_op jit(solution)/shard_map/psum | solution.py:62
  622.6 1.2 fusion.39
  624.0 2.3 convolution_add_fusion
  626.3 1.1 select_bitcast_fusion.2
  627.4 6.7 collective-permute-start.13
  634.9 3.6 collective-permute-start.15
  638.7 1.2 broadcast.85.clone.11
  639.9 1.9 dynamic_update_slice.61
  641.8 1.1 collective-permute-done.14
  642.9 1.2 broadcast.85.clone.10
  644.1 1.9 dynamic_update_slice.62
  646.0 1.2 broadcast.85.clone.9
  647.2 1.9 dynamic_update_slice.63
  649.1 3.7 multiply_reduce_fusion
  652.8 78.6 %psum.71 = f32[128]{0:T(128)} all-reduce(f32[128]{0:T(128)S(1)} %get-tuple-element.8), channel_id=1, replica_groups=mesh['cluster'=8,'sub'=32] {'cluster','sub'}, use_global_device_ids=true, to_apply=%region_16.17 | all-reduce | flops 128 | bytes 1024 | tf_op jit(solution)/shard_map/psum | solution.py:66
  732.1 3.3 subtract_bitcast_fusion
  735.4 2.6 copy.13
  738.0 1.3 copy.14
  (105 shorter events, 20.7 us)
Async XLA Ops:
  7.2 36.8 %copy-start = (f32[1,1,48,2048]{3,2,1,0:T(8,128)S(1)}, f32[1,1,48,2048]{3,2,1,0:T(8,128)}, u32[]{:S(2)}) copy-start(f32[1,1,48,2048]{3,2,1,0:T(8,128)} %param.7) | copy-start | bytes 1179652
  7.2 108.8 %all-reduce.9.cloned.1.call-start = ((), (), s32[]{:S(2)}) async-start(), calls=%async_computation | async-start | bytes 131072 | tf_op jit(solution)/shard_map/psum | solution.py:62
  16.1 5.5 copy-start.4
  18.1 14.6 %collective-permute-start.1 = (f32[512,128]{0,1:T(8,128)S(1)}, f32[512,128]{0,1:T(8,128)S(1)}, u32[]{:S(2)}, u32[]{:S(2)}) collective-permute-start(f32[512,128]{0,1:T(8,128)S(1)} %bitcast_select_fusion.2), channel_id=1, source_target_pairs={{31,0},{0,1},{1,2},{2,3},{3,4},{4,5},{5,6},{6,7},{7,8},{8,9},{9,10... | collective-permute-start | bytes 786440 | tf_op jit(solution)/shard_map/ppermute | solution.py:15
  21.0 14.7 %collective-permute-start.2 = (f32[512,128]{0,1:T(8,128)S(1)}, f32[512,128]{0,1:T(8,128)}, u32[]{:S(2)}, u32[]{:S(2)}) collective-permute-start(f32[512,128]{0,1:T(8,128)S(1)} %bitcast_select_fusion.1), channel_id=1, source_target_pairs={{1,0},{2,1},{3,2},{4,3},{5,4},{6,5},{7,6},{8,7},{9,8},{10,9},{11,1... | collective-permute-start | bytes 786440 | tf_op jit(solution)/shard_map/ppermute | solution.py:15
  22.6 9.4 %copy-start.7 = (pred[512]{0:T(512)(128)(4,1)}, pred[512]{0:T(512)(128)(4,1)S(1)}, u32[]{:S(2)}) copy-start(pred[512]{0:T(512)(128)(4,1)S(1)} %iota_compare_fusion.5) | copy-start | bytes 1540
  22.6 16.2 %collective-permute-start.3 = (f32[512,128]{0,1:T(8,128)S(1)}, f32[512,128]{0,1:T(8,128)S(1)}, u32[]{:S(2)}, u32[]{:S(2)}) collective-permute-start(f32[512,128]{0,1:T(8,128)S(1)} %fusion.38), channel_id=1, source_target_pairs={{2,0},{3,1},{4,2},{5,3},{6,4},{7,5},{8,6},{9,7},{10,8},{11,9},{12,... | collective-permute-start | bytes 786440 | tf_op jit(solution)/shard_map/ppermute | solution.py:15
  28.1 8.7 %copy-start.11 = (pred[512]{0:T(512)(128)(4,1)}, pred[512]{0:T(512)(128)(4,1)S(1)}, u32[]{:S(2)}) copy-start(pred[512]{0:T(512)(128)(4,1)S(1)} %iota_compare_fusion.8) | copy-start | bytes 1540
  28.2 13.6 %collective-permute-start = (f32[512,128]{0,1:T(8,128)S(1)}, f32[512,128]{0,1:T(8,128)S(1)}, u32[]{:S(2)}, u32[]{:S(2)}) collective-permute-start(f32[512,128]{0,1:T(8,128)S(1)} %bitcast_select_fusion.3), channel_id=1, source_target_pairs={{30,0},{31,1},{0,2},{1,3},{2,4},{3,5},{4,6},{5,7},{6,8},{7,9},{8,1... | collective-permute-start | bytes 786440 | tf_op jit(solution)/shard_map/ppermute | solution.py:15
  44.0 1.0 copy-start.6
  44.0 72.0 %copy-start.5 = (f32[1,128,128]{2,1,0:T(8,128)S(1)}, f32[1,128,128]{2,1,0:T(8,128)}, u32[]{:S(2)}) copy-start(f32[1,128,128]{2,1,0:T(8,128)} %param.8) | copy-start | bytes 196612
  45.9 323.3 %all-reduce.11.cloned.1.call-start = ((), (), s32[]{:S(2)}) async-start(), calls=%async_computation.1 | async-start | bytes 131072 | tf_op jit(solution)/shard_map/psum | solution.py:62
  118.4 6.3 copy-start.12
  124.7 7.8 %copy-start.8 = (pred[512]{0:T(512)(128)(4,1)S(1)}, pred[512]{0:T(512)(128)(4,1)}, u32[]{:S(2)}) copy-start(pred[512]{0:T(512)(128)(4,1)} %copy-done.7) | copy-start | bytes 1540
  125.8 10.9 %collective-permute-start.5 = (f32[512,128]{0,1:T(8,128)S(1)}, f32[512,128]{0,1:T(8,128)S(1)}, u32[]{:S(2)}, u32[]{:S(2)}) collective-permute-start(f32[512,128]{0,1:T(8,128)S(1)} %get-tuple-element.23), channel_id=1, source_target_pairs={{31,0},{0,1},{1,2},{2,3},{3,4},{4,5},{5,6},{6,7},{7,8},{8,9},{9,10... | collective-permute-start | bytes 786440 | tf_op jit(solution)/shard_map/ppermute | solution.py:15
  132.5 8.6 %collective-permute-start.6 = (f32[512,128]{0,1:T(8,128)}, f32[512,128]{0,1:T(8,128)S(1)}, u32[]{:S(2)}, u32[]{:S(2)}) collective-permute-start(f32[512,128]{0,1:T(8,128)} %get-tuple-element.22), channel_id=1, source_target_pairs={{1,0},{2,1},{3,2},{4,3},{5,4},{6,5},{7,6},{8,7},{9,8},{10,9},{11,1... | collective-permute-start | bytes 786440 | tf_op jit(solution)/shard_map/ppermute | solution.py:15
  132.6 11.6 %collective-permute-start.7 = (f32[512,128]{0,1:T(8,128)S(1)}, f32[512,128]{0,1:T(8,128)S(1)}, u32[]{:S(2)}, u32[]{:S(2)}) collective-permute-start(f32[512,128]{0,1:T(8,128)S(1)} %slice_select_fusion.2), channel_id=1, source_target_pairs={{2,0},{3,1},{4,2},{5,3},{6,4},{7,5},{8,6},{9,7},{10,8},{11,9},{12,... | collective-permute-start | bytes 786440 | tf_op jit(solution)/shard_map/ppermute | solution.py:15
  136.7 10.5 %collective-permute-start.4 = (f32[512,128]{0,1:T(8,128)}, f32[512,128]{0,1:T(8,128)}, u32[]{:S(2)}, u32[]{:S(2)}) collective-permute-start(f32[512,128]{0,1:T(8,128)} %get-tuple-element.21), channel_id=1, source_target_pairs={{30,0},{31,1},{0,2},{1,3},{2,4},{3,5},{4,6},{5,7},{6,8},{7,9},{8,1... | collective-permute-start | bytes 786440 | tf_op jit(solution)/shard_map/ppermute | solution.py:15
  228.7 0.6 copy-start.15
  302.0 0.5 copy-start.20
  305.5 317.1 %all-reduce.13.cloned.1.call-start = ((), (), s32[]{:S(2)}) async-start(), calls=%async_computation.2 | async-start | bytes 131072 | tf_op jit(solution)/shard_map/psum | solution.py:62
  370.4 2.5 copy-start.13
  372.9 7.9 %copy-start.2 = (f32[128,2048]{1,0:T(8,128)}, f32[128,2048]{1,0:T(8,128)S(1)}, u32[]{:S(2)}) copy-start(f32[128,2048]{1,0:T(8,128)S(1)} %convolution_add_fusion.1) | copy-start | bytes 3145732
  373.0 7.9 %copy-start.9 = (pred[512]{0:T(512)(128)(4,1)S(1)}, pred[512]{0:T(512)(128)(4,1)}, u32[]{:S(2)}) copy-start(pred[512]{0:T(512)(128)(4,1)} %copy-done.7) | copy-start | bytes 1540
  374.1 11.2 %collective-permute-start.9 = (f32[512,128]{0,1:T(8,128)S(1)}, f32[512,128]{0,1:T(8,128)}, u32[]{:S(2)}, u32[]{:S(2)}) collective-permute-start(f32[512,128]{0,1:T(8,128)S(1)} %get-tuple-element.20), channel_id=1, source_target_pairs={{31,0},{0,1},{1,2},{2,3},{3,4},{4,5},{5,6},{6,7},{7,8},{8,9},{9,10... | collective-permute-start | bytes 786440 | tf_op jit(solution)/shard_map/ppermute | solution.py:15
  380.8 8.8 %collective-permute-start.10 = (f32[512,128]{0,1:T(8,128)}, f32[512,128]{0,1:T(8,128)}, u32[]{:S(2)}, u32[]{:S(2)}) collective-permute-start(f32[512,128]{0,1:T(8,128)} %get-tuple-element.19), channel_id=1, source_target_pairs={{1,0},{2,1},{3,2},{4,3},{5,4},{6,5},{7,6},{8,7},{9,8},{10,9},{11,1... | collective-permute-start | bytes 786440 | tf_op jit(solution)/shard_map/ppermute | solution.py:15
  381.5 11.1 %collective-permute-start.11 = (f32[512,128]{0,1:T(8,128)}, f32[512,128]{0,1:T(8,128)}, u32[]{:S(2)}, u32[]{:S(2)}) collective-permute-start(f32[512,128]{0,1:T(8,128)} %slice_select_fusion.1), channel_id=1, source_target_pairs={{2,0},{3,1},{4,2},{5,3},{6,4},{7,5},{8,6},{9,7},{10,8},{11,9},{12,... | collective-permute-start | bytes 786440 | tf_op jit(solution)/shard_map/ppermute | solution.py:15
  385.1 10.7 %collective-permute-start.8 = (f32[512,128]{0,1:T(8,128)}, f32[512,128]{0,1:T(8,128)}, u32[]{:S(2)}, u32[]{:S(2)}) collective-permute-start(f32[512,128]{0,1:T(8,128)} %get-tuple-element.18), channel_id=1, source_target_pairs={{30,0},{31,1},{0,2},{1,3},{2,4},{3,5},{4,6},{5,7},{6,8},{7,9},{8,1... | collective-permute-start | bytes 786440 | tf_op jit(solution)/shard_map/ppermute | solution.py:15
  479.3 3.0 copy-start.17
  554.8 0.6 copy-start.19
  623.8 2.5 copy-start.14
  626.3 7.9 %copy-start.1 = (f32[128,2048]{1,0:T(8,128)}, f32[128,2048]{1,0:T(8,128)S(1)}, u32[]{:S(2)}) copy-start(f32[128,2048]{1,0:T(8,128)S(1)} %convolution_add_fusion) | copy-start | bytes 3145732
  626.3 7.9 %copy-start.10 = (pred[512]{0:T(512)(128)(4,1)S(1)}, pred[512]{0:T(512)(128)(4,1)}, u32[]{:S(2)}) copy-start(pred[512]{0:T(512)(128)(4,1)} %copy-done.7) | copy-start | bytes 1540
  627.4 11.3 %collective-permute-start.13 = (f32[512,128]{0,1:T(8,128)S(1)}, f32[512,128]{0,1:T(8,128)}, u32[]{:S(2)}, u32[]{:S(2)}) collective-permute-start(f32[512,128]{0,1:T(8,128)S(1)} %get-tuple-element.17), channel_id=1, source_target_pairs={{31,0},{0,1},{1,2},{2,3},{3,4},{4,5},{5,6},{6,7},{7,8},{8,9},{9,10... | collective-permute-start | bytes 786440 | tf_op jit(solution)/shard_map/ppermute | solution.py:15
  634.1 8.7 %collective-permute-start.14 = (f32[512,128]{0,1:T(8,128)}, f32[512,128]{0,1:T(8,128)}, u32[]{:S(2)}, u32[]{:S(2)}) collective-permute-start(f32[512,128]{0,1:T(8,128)} %get-tuple-element.16), channel_id=1, source_target_pairs={{1,0},{2,1},{3,2},{4,3},{5,4},{6,5},{7,6},{8,7},{9,8},{10,9},{11,1... | collective-permute-start | bytes 786440 | tf_op jit(solution)/shard_map/ppermute | solution.py:15
  634.9 11.1 %collective-permute-start.15 = (f32[512,128]{0,1:T(8,128)}, f32[512,128]{0,1:T(8,128)}, u32[]{:S(2)}, u32[]{:S(2)}) collective-permute-start(f32[512,128]{0,1:T(8,128)} %slice_select_fusion), channel_id=1, source_target_pairs={{2,0},{3,1},{4,2},{5,3},{6,4},{7,5},{8,6},{9,7},{10,8},{11,9},{12,... | collective-permute-start | bytes 786440 | tf_op jit(solution)/shard_map/ppermute | solution.py:15
  638.5 10.7 %collective-permute-start.12 = (f32[512,128]{0,1:T(8,128)}, f32[512,128]{0,1:T(8,128)}, u32[]{:S(2)}, u32[]{:S(2)}) collective-permute-start(f32[512,128]{0,1:T(8,128)} %get-tuple-element.15), channel_id=1, source_target_pairs={{30,0},{31,1},{0,2},{1,3},{2,4},{3,5},{4,6},{5,7},{6,8},{7,9},{8,1... | collective-permute-start | bytes 786440 | tf_op jit(solution)/shard_map/ppermute | solution.py:15
  649.1 83.0 %copy-start.16 = (f32[128]{0:T(128)S(1)}, f32[128]{0:T(128)}, u32[]{:S(2)}) copy-start(f32[128]{0:T(128)} %copy-done.15) | copy-start | bytes 1540
  649.1 83.0 %copy-start.18 = (f32[128]{0:T(128)S(1)}, f32[128]{0:T(128)}, u32[]{:S(2)}) copy-start(f32[128]{0:T(128)} %copy-done.17) | copy-start | bytes 1540
  735.4 2.6 copy-start.3
Sparse Core Ops, SparseCore 0:
  46.1 69.9 all-reduce.8
  305.6 63.6 all-reduce.10
  558.8 63.7 all-reduce.12
where the time goes:
time: 756 us; the launch traced here: 746 us
  blocking collectives  381 us (50%)
  waiting for transfers between devices  187 us (25%)
  local copies, waits for them, and re-layouts  45.1 us (6%)
  starting transfers between devices  40.2 us (5%)
  matrix products  36 us (5%)
  other arithmetic  33.2 us (4%)
  between operations  23.7 us (3%)
    psum x3, blocking collectives, local(): lax.psum(jnp.sum(residual * residual, axis=0), ('cluster', 'sub'))  224 us
    psum x3, waiting for transfers between devices, local(): coarse_total = lax.psum(coarse_part, 'cluster')  183 us
    psum x2, blocking collectives, local(): curvature = lax.psum(jnp.sum(direction * image, axis=0), ('cluster', 'sub'))  157 us
    ppermute x16, starting transfers between devices, passed_along(): return lax.ppermute(block, axis, route)  40 us
    dynamic_update_slice x12, local copies, waits for them, and re-layouts, insert_run(): lax.dynamic_update_slice_in_dim(padded, run_block, start_row, 0)[:dual_rows]  22.4 us
    dot_general x3, matrix products, local(): jnp.dot(operator, direction.astype(jnp.bfloat16), preferred_element_type=...  20.7 us
  transfers between devices with their start and end apart: 19, of which 6 were waited for; matrix products, arithmetic and copies ran while one was open for 7% of the time, Pallas kernels for 0%

commit v1 on v0

--- a/solution.py
+++ b/solution.py
@@ -63,7 +63,9 @@
         coarse_solution = jnp.dot(inverse, coarse_total, precision=highest)
         corner_back = jnp.dot(onehot, coarse_solution, precision=highest)
         image = assemble(local_part + jnp.dot(coupling.T, corner_back, precision=highest))
-        curvature = lax.psum(jnp.sum(direction * image, axis=0), ("cluster", "sub"))
+        curvature = jnp.sum(
+            lax.all_gather(jnp.sum(direction * image, axis=0), ("cluster", "sub")), axis=0
+        )
         step_size = norm_now / curvature
         multipliers = multipliers + step_size * direction
         residual = residual - step_size * image

time: 756 us -> 779 us (1.030)
  blocking collectives: 381 us -> 402 us
    all_gather x0 -> x3, blocking collectives: none -> 181 us  [local(): lax.all_gather(jnp.sum(direction * image, axis=0), ('cluster', 'sub'))]
    psum x2 -> x0, blocking collectives: 157 us -> none  [local(): curvature = lax.psum(jnp.sum(direction * image, axis=0), ('cluster', 'sub'))]
where the time goes in v1:
time: 779 us; the launch traced here: 770 us
  blocking collectives  402 us (52%)
  waiting for transfers between devices  186 us (24%)
  local copies, waits for them, and re-layouts  45.2 us (6%)
  starting transfers between devices  40.2 us (5%)
  matrix products  36 us (5%)
  other arithmetic  35.9 us (5%)
  between operations  24.2 us (3%)
    psum x3, blocking collectives, local(): lax.psum(jnp.sum(residual * residual, axis=0), ('cluster', 'sub'))  222 us
    psum x3, waiting for transfers between devices, local(): coarse_total = lax.psum(coarse_part, 'cluster')  182 us
    all_gather x3, blocking collectives, local(): lax.all_gather(jnp.sum(direction * image, axis=0), ('cluster', 'sub'))  181 us
    ppermute x16, starting transfers between devices, passed_along(): return lax.ppermute(block, axis, route)  40 us
    dynamic_update_slice x12, local copies, waits for them, and re-layouts, insert_run(): lax.dynamic_update_slice_in_dim(padded, run_block, start_row, 0)[:dual_rows]  22.4 us
    dot_general x3, matrix products, local(): jnp.dot(operator, direction.astype(jnp.bfloat16), preferred_element_type=...  20.7 us
  transfers between devices with their start and end apart: 19, of which 6 were waited for; matrix products, arithmetic and copies ran while one was open for 7% of the time, Pallas kernels for 0%

profile of v1, /device:TPU:1, one launch (start us, length us, event | category | flops | bytes accessed | tf_op | source)
XLA Modules:
  0.0 769.5 jit_solution(7975096518692466637)
XLA Ops:
  7.2 1.3 fusion.62
  15.2 1.2 constant_dynamic-slice_fusion.1
  17.2 1.2 iota_compare_fusion.6
  18.4 2.8 collective-permute-start.1
  23.0 4.8 collective-permute-start.3
  33.2 1.2 broadcast.85.clone.2
  34.4 1.8 dynamic_update_slice.49
  36.3 1.2 broadcast.85.clone.1
  37.5 1.9 dynamic_update_slice.50
  39.4 1.2 broadcast.85.clone
  40.6 1.8 dynamic_update_slice.51
  42.4 2.2 fusion.12
  46.6 70.0 %all-reduce.8.cloned.1.call-done = f32[128,128]{1,0:T(8,128)} async-done(((f32[128,128]{1,0:T(8,128)}), f32[128,128]{1,0:T(8,128)}) %all-reduce.8.cloned.1.call-update) | async-done | bytes 65552 | tf_op jit(solution)/shard_map/psum | solution.py:62
  119.1 6.3 fusion.6
  126.4 6.7 collective-permute-start.5
  133.2 4.1 collective-permute-start.7
  137.3 1.2 broadcast.85.clone.5
  138.5 1.8 dynamic_update_slice.53
  140.3 1.4 collective-permute-done.6
  141.7 1.2 broadcast.85.clone.4
  142.9 1.9 dynamic_update_slice.54
  144.8 1.2 broadcast.85.clone.3
  146.0 1.8 dynamic_update_slice.55
  147.8 2.8 multiply_reduce_fusion.4
  150.6 57.8 %all-gather.3 = f32[256,1,128]{2,1,0:T(1,128)S(1)} all-gather(f32[1,1,128]{2,1,0:T(1,128)S(1)} %bitcast.111), channel_id=2, replica_groups=mesh['cluster'=8,'sub'=32] {'cluster','sub'}, dimensions={0}, use_global_device_ids=true | all-gather | bytes 131584 | tf_op jit(solution)/shard_map/all_gather | solution.py:67
  208.4 73.7 %psum.42 = f32[128]{0:T(128)S(1)} all-reduce(f32[128]{0:T(128)} %get-tuple-element.7), channel_id=1, replica_groups=mesh['cluster'=8,'sub'=32] {'cluster','sub'}, use_global_device_ids=true, to_apply=%region_3.4 | all-reduce | flops 128 | bytes 1024 | tf_op jit(solution)/shard_map/psum | solution.py:55
  283.3 73.6 %psum.44 = f32[128]{0:T(128)S(1)} all-reduce(f32[128]{0:T(128)S(1)} %multiply_reduce_fusion.3), channel_id=1, replica_groups=mesh['cluster'=8,'sub'=32] {'cluster','sub'}, use_global_device_ids=true, to_apply=%region_8.9 | all-reduce | flops 128 | bytes 1024 | tf_op jit(solution)/shard_map/psum | solution.py:72
  360.4 7.2 fusion.2
  367.6 55.9 %all-reduce.10.cloned.1.call-done = f32[128,128]{1,0:T(8,128)} async-done(((f32[128,128]{1,0:T(8,128)}), f32[128,128]{1,0:T(8,128)}) %all-reduce.10.cloned.1.call-update) | async-done | bytes 65552 | tf_op jit(solution)/shard_map/psum | solution.py:62
  423.5 1.2 fusion.41
  424.9 2.3 convolution_add_fusion.1
  428.3 6.7 collective-permute-start.9
  435.8 3.6 collective-permute-start.11
  439.5 1.2 broadcast.85.clone.8
  440.7 1.9 dynamic_update_slice.57
  442.6 1.1 collective-permute-done.10
  443.8 1.2 broadcast.85.clone.7
  445.0 1.9 dynamic_update_slice.58
  446.9 1.2 broadcast.85.clone.6
  448.1 1.9 dynamic_update_slice.59
  450.0 3.7 multiply_reduce_fusion.2
  453.7 61.4 %all-gather.4 = f32[256,1,128]{2,1,0:T(1,128)} all-gather(f32[1,1,128]{2,1,0:T(1,128)S(1)} %bitcast.113), channel_id=3, replica_groups=mesh['cluster'=8,'sub'=32] {'cluster','sub'}, dimensions={0}, use_global_device_ids=true | all-gather | bytes 131584 | tf_op jit(solution)/shard_map/all_gather | solution.py:67
  515.0 1.7 reduce_sum.96
  517.4 3.0 multiply_reduce_fusion.1
  520.4 74.5 %psum.46 = f32[128]{0:T(128)S(1)} all-reduce(f32[128]{0:T(128)} %get-tuple-element.10), channel_id=1, replica_groups=mesh['cluster'=8,'sub'=32] {'cluster','sub'}, use_global_device_ids=true, to_apply=%region_13.14 | all-reduce | flops 128 | bytes 1024 | tf_op jit(solution)/shard_map/psum | solution.py:72
  595.5 1.4 multiply_add_fusion
  598.8 7.2 fusion
  606.1 56.0 %all-reduce.12.cloned.1.call-done = f32[128,128]{1,0:T(8,128)} async-done(((f32[128,128]{1,0:T(8,128)}), f32[128,128]{1,0:T(8,128)}) %all-reduce.12.cloned.1.call-update) | async-done | bytes 65552 | tf_op jit(solution)/shard_map/psum | solution.py:62
  662.1 1.2 fusion.39
  663.5 2.3 convolution_add_fusion
  666.9 6.7 collective-permute-start.13
  674.4 3.6 collective-permute-start.15
  678.2 1.2 broadcast.85.clone.11
  679.4 1.9 dynamic_update_slice.61
  682.4 1.2 broadcast.85.clone.10
  683.6 1.9 dynamic_update_slice.62
  685.5 1.2 broadcast.85.clone.9
  686.7 1.9 dynamic_update_slice.63
  688.6 3.7 multiply_reduce_fusion
  692.3 61.4 %all-gather.5 = f32[256,1,128]{2,1,0:T(1,128)} all-gather(f32[1,1,128]{2,1,0:T(1,128)S(1)} %bitcast.112), channel_id=4, replica_groups=mesh['cluster'=8,'sub'=32] {'cluster','sub'}, dimensions={0}, use_global_device_ids=true | all-gather | bytes 131584 | tf_op jit(solution)/shard_map/all_gather | solution.py:67
  753.7 1.2 reduce_sum.99
  755.5 3.3 subtract_bitcast_fusion
  758.8 2.6 copy.20
  761.5 1.3 copy.21
  (109 shorter events, 24.5 us)
Async XLA Ops:
  7.2 37.4 %copy-start = (f32[1,1,48,2048]{3,2,1,0:T(8,128)S(1)}, f32[1,1,48,2048]{3,2,1,0:T(8,128)}, u32[]{:S(2)}) copy-start(f32[1,1,48,2048]{3,2,1,0:T(8,128)} %param.7) | copy-start | bytes 1179652
  7.2 109.5 %all-reduce.8.cloned.1.call-start = ((), (), s32[]{:S(2)}) async-start(), calls=%async_computation | async-start | bytes 131072 | tf_op jit(solution)/shard_map/psum | solution.py:62
  16.4 5.5 copy-start.4
  18.4 14.8 %collective-permute-start.1 = (f32[512,128]{0,1:T(8,128)S(1)}, f32[512,128]{0,1:T(8,128)S(1)}, u32[]{:S(2)}, u32[]{:S(2)}) collective-permute-start(f32[512,128]{0,1:T(8,128)S(1)} %bitcast_select_fusion.2), channel_id=1, source_target_pairs={{31,0},{0,1},{1,2},{2,3},{3,4},{4,5},{5,6},{6,7},{7,8},{8,9},{9,10... | collective-permute-start | bytes 786440 | tf_op jit(solution)/shard_map/ppermute | solution.py:15
  21.4 14.9 %collective-permute-start.2 = (f32[512,128]{0,1:T(8,128)S(1)}, f32[512,128]{0,1:T(8,128)}, u32[]{:S(2)}, u32[]{:S(2)}) collective-permute-start(f32[512,128]{0,1:T(8,128)S(1)} %bitcast_select_fusion.1), channel_id=1, source_target_pairs={{1,0},{2,1},{3,2},{4,3},{5,4},{6,5},{7,6},{8,7},{9,8},{10,9},{11,1... | collective-permute-start | bytes 786440 | tf_op jit(solution)/shard_map/ppermute | solution.py:15
  22.9 9.6 %copy-start.7 = (pred[512]{0:T(512)(128)(4,1)}, pred[512]{0:T(512)(128)(4,1)S(1)}, u32[]{:S(2)}) copy-start(pred[512]{0:T(512)(128)(4,1)S(1)} %iota_compare_fusion.5) | copy-start | bytes 1540
  23.0 16.4 %collective-permute-start.3 = (f32[512,128]{0,1:T(8,128)S(1)}, f32[512,128]{0,1:T(8,128)S(1)}, u32[]{:S(2)}, u32[]{:S(2)}) collective-permute-start(f32[512,128]{0,1:T(8,128)S(1)} %fusion.38), channel_id=1, source_target_pairs={{2,0},{3,1},{4,2},{5,3},{6,4},{7,5},{8,6},{9,7},{10,8},{11,9},{12,... | collective-permute-start | bytes 786440 | tf_op jit(solution)/shard_map/ppermute | solution.py:15
  28.5 9.0 %copy-start.11 = (pred[512]{0:T(512)(128)(4,1)}, pred[512]{0:T(512)(128)(4,1)S(1)}, u32[]{:S(2)}) copy-start(pred[512]{0:T(512)(128)(4,1)S(1)} %iota_compare_fusion.8) | copy-start | bytes 1540
  28.6 13.8 %collective-permute-start = (f32[512,128]{0,1:T(8,128)S(1)}, f32[512,128]{0,1:T(8,128)S(1)}, u32[]{:S(2)}, u32[]{:S(2)}) collective-permute-start(f32[512,128]{0,1:T(8,128)S(1)} %bitcast_select_fusion.3), channel_id=1, source_target_pairs={{30,0},{31,1},{0,2},{1,3},{2,4},{3,5},{4,6},{5,7},{6,8},{7,9},{8,1... | collective-permute-start | bytes 786440 | tf_op jit(solution)/shard_map/ppermute | solution.py:15
  44.6 1.0 copy-start.6
  44.6 72.0 %copy-start.5 = (f32[1,128,128]{2,1,0:T(8,128)S(1)}, f32[1,128,128]{2,1,0:T(8,128)}, u32[]{:S(2)}) copy-start(f32[1,128,128]{2,1,0:T(8,128)} %param.8) | copy-start | bytes 196612
  46.6 376.9 %all-reduce.10.cloned.1.call-start = ((), (), s32[]{:S(2)}) async-start(), calls=%async_computation.1 | async-start | bytes 131072 | tf_op jit(solution)/shard_map/psum | solution.py:62
  119.0 6.3 copy-start.12
  125.3 7.8 %copy-start.8 = (pred[512]{0:T(512)(128)(4,1)S(1)}, pred[512]{0:T(512)(128)(4,1)}, u32[]{:S(2)}) copy-start(pred[512]{0:T(512)(128)(4,1)} %copy-done.7) | copy-start | bytes 1540
  126.4 10.9 %collective-permute-start.5 = (f32[512,128]{0,1:T(8,128)S(1)}, f32[512,128]{0,1:T(8,128)S(1)}, u32[]{:S(2)}, u32[]{:S(2)}) collective-permute-start(f32[512,128]{0,1:T(8,128)S(1)} %get-tuple-element.23), channel_id=1, source_target_pairs={{31,0},{0,1},{1,2},{2,3},{3,4},{4,5},{5,6},{6,7},{7,8},{8,9},{9,10... | collective-permute-start | bytes 786440 | tf_op jit(solution)/shard_map/ppermute | solution.py:15
  133.1 8.6 %collective-permute-start.6 = (f32[512,128]{0,1:T(8,128)}, f32[512,128]{0,1:T(8,128)S(1)}, u32[]{:S(2)}, u32[]{:S(2)}) collective-permute-start(f32[512,128]{0,1:T(8,128)} %get-tuple-element.22), channel_id=1, source_target_pairs={{1,0},{2,1},{3,2},{4,3},{5,4},{6,5},{7,6},{8,7},{9,8},{10,9},{11,1... | collective-permute-start | bytes 786440 | tf_op jit(solution)/shard_map/ppermute | solution.py:15
  133.2 11.6 %collective-permute-start.7 = (f32[512,128]{0,1:T(8,128)S(1)}, f32[512,128]{0,1:T(8,128)S(1)}, u32[]{:S(2)}, u32[]{:S(2)}) collective-permute-start(f32[512,128]{0,1:T(8,128)S(1)} %slice_select_fusion.2), channel_id=1, source_target_pairs={{2,0},{3,1},{4,2},{5,3},{6,4},{7,5},{8,6},{9,7},{10,8},{11,9},{12,... | collective-permute-start | bytes 786440 | tf_op jit(solution)/shard_map/ppermute | solution.py:15
  137.3 10.5 %collective-permute-start.4 = (f32[512,128]{0,1:T(8,128)}, f32[512,128]{0,1:T(8,128)}, u32[]{:S(2)}, u32[]{:S(2)}) collective-permute-start(f32[512,128]{0,1:T(8,128)} %get-tuple-element.21), channel_id=1, source_target_pairs={{30,0},{31,1},{0,2},{1,3},{2,4},{3,5},{4,6},{5,7},{6,8},{7,9},{8,1... | collective-permute-start | bytes 786440 | tf_op jit(solution)/shard_map/ppermute | solution.py:15
  282.4 0.6 copy-start.15
  356.9 0.5 copy-start.20
  360.3 301.8 %all-reduce.12.cloned.1.call-start = ((), (), s32[]{:S(2)}) async-start(), calls=%async_computation.2 | async-start | bytes 131072 | tf_op jit(solution)/shard_map/psum | solution.py:62
  424.7 2.5 copy-start.13
  427.2 7.9 %copy-start.2 = (f32[128,2048]{1,0:T(8,128)}, f32[128,2048]{1,0:T(8,128)S(1)}, u32[]{:S(2)}) copy-start(f32[128,2048]{1,0:T(8,128)S(1)} %convolution_add_fusion.1) | copy-start | bytes 3145732
  427.2 7.9 %copy-start.9 = (pred[512]{0:T(512)(128)(4,1)S(1)}, pred[512]{0:T(512)(128)(4,1)}, u32[]{:S(2)}) copy-start(pred[512]{0:T(512)(128)(4,1)} %copy-done.7) | copy-start | bytes 1540
  428.3 11.2 %collective-permute-start.9 = (f32[512,128]{0,1:T(8,128)S(1)}, f32[512,128]{0,1:T(8,128)}, u32[]{:S(2)}, u32[]{:S(2)}) collective-permute-start(f32[512,128]{0,1:T(8,128)S(1)} %get-tuple-element.20), channel_id=1, source_target_pairs={{31,0},{0,1},{1,2},{2,3},{3,4},{4,5},{5,6},{6,7},{7,8},{8,9},{9,10... | collective-permute-start | bytes 786440 | tf_op jit(solution)/shard_map/ppermute | solution.py:15
  435.0 8.8 %collective-permute-start.10 = (f32[512,128]{0,1:T(8,128)}, f32[512,128]{0,1:T(8,128)}, u32[]{:S(2)}, u32[]{:S(2)}) collective-permute-start(f32[512,128]{0,1:T(8,128)} %get-tuple-element.19), channel_id=1, source_target_pairs={{1,0},{2,1},{3,2},{4,3},{5,4},{6,5},{7,6},{8,7},{9,8},{10,9},{11,1... | collective-permute-start | bytes 786440 | tf_op jit(solution)/shard_map/ppermute | solution.py:15
  435.8 11.1 %collective-permute-start.11 = (f32[512,128]{0,1:T(8,128)}, f32[512,128]{0,1:T(8,128)}, u32[]{:S(2)}, u32[]{:S(2)}) collective-permute-start(f32[512,128]{0,1:T(8,128)} %slice_select_fusion.1), channel_id=1, source_target_pairs={{2,0},{3,1},{4,2},{5,3},{6,4},{7,5},{8,6},{9,7},{10,8},{11,9},{12,... | collective-permute-start | bytes 786440 | tf_op jit(solution)/shard_map/ppermute | solution.py:15
  439.3 10.6 %collective-permute-start.8 = (f32[512,128]{0,1:T(8,128)}, f32[512,128]{0,1:T(8,128)}, u32[]{:S(2)}, u32[]{:S(2)}) collective-permute-start(f32[512,128]{0,1:T(8,128)} %get-tuple-element.18), channel_id=1, source_target_pairs={{30,0},{31,1},{0,2},{1,3},{2,4},{3,5},{4,6},{5,7},{6,8},{7,9},{8,1... | collective-permute-start | bytes 786440 | tf_op jit(solution)/shard_map/ppermute | solution.py:15
  517.4 3.0 copy-start.17
  594.9 0.6 copy-start.19
  663.2 2.5 copy-start.14
  665.8 7.9 %copy-start.1 = (f32[128,2048]{1,0:T(8,128)}, f32[128,2048]{1,0:T(8,128)S(1)}, u32[]{:S(2)}) copy-start(f32[128,2048]{1,0:T(8,128)S(1)} %convolution_add_fusion) | copy-start | bytes 3145732
  665.8 7.9 %copy-start.10 = (pred[512]{0:T(512)(128)(4,1)S(1)}, pred[512]{0:T(512)(128)(4,1)}, u32[]{:S(2)}) copy-start(pred[512]{0:T(512)(128)(4,1)} %copy-done.7) | copy-start | bytes 1540
  666.9 11.3 %collective-permute-start.13 = (f32[512,128]{0,1:T(8,128)S(1)}, f32[512,128]{0,1:T(8,128)}, u32[]{:S(2)}, u32[]{:S(2)}) collective-permute-start(f32[512,128]{0,1:T(8,128)S(1)} %get-tuple-element.17), channel_id=1, source_target_pairs={{31,0},{0,1},{1,2},{2,3},{3,4},{4,5},{5,6},{6,7},{7,8},{8,9},{9,10... | collective-permute-start | bytes 786440 | tf_op jit(solution)/shard_map/ppermute | solution.py:15
  673.6 8.8 %collective-permute-start.14 = (f32[512,128]{0,1:T(8,128)}, f32[512,128]{0,1:T(8,128)}, u32[]{:S(2)}, u32[]{:S(2)}) collective-permute-start(f32[512,128]{0,1:T(8,128)} %get-tuple-element.16), channel_id=1, source_target_pairs={{1,0},{2,1},{3,2},{4,3},{5,4},{6,5},{7,6},{8,7},{9,8},{10,9},{11,1... | collective-permute-start | bytes 786440 | tf_op jit(solution)/shard_map/ppermute | solution.py:15
  674.4 11.2 %collective-permute-start.15 = (f32[512,128]{0,1:T(8,128)}, f32[512,128]{0,1:T(8,128)}, u32[]{:S(2)}, u32[]{:S(2)}) collective-permute-start(f32[512,128]{0,1:T(8,128)} %slice_select_fusion), channel_id=1, source_target_pairs={{2,0},{3,1},{4,2},{5,3},{6,4},{7,5},{8,6},{9,7},{10,8},{11,9},{12,... | collective-permute-start | bytes 786440 | tf_op jit(solution)/shard_map/ppermute | solution.py:15
  677.9 10.7 %collective-permute-start.12 = (f32[512,128]{0,1:T(8,128)}, f32[512,128]{0,1:T(8,128)}, u32[]{:S(2)}, u32[]{:S(2)}) collective-permute-start(f32[512,128]{0,1:T(8,128)} %get-tuple-element.15), channel_id=1, source_target_pairs={{30,0},{31,1},{0,2},{1,3},{2,4},{3,5},{4,6},{5,7},{6,8},{7,9},{8,1... | collective-permute-start | bytes 786440 | tf_op jit(solution)/shard_map/ppermute | solution.py:15
  688.6 66.9 %copy-start.16 = (f32[128]{0:T(128)S(1)}, f32[128]{0:T(128)}, u32[]{:S(2)}) copy-start(f32[128]{0:T(128)} %copy-done.15) | copy-start | bytes 1540
  688.6 66.9 %copy-start.18 = (f32[128]{0:T(128)S(1)}, f32[128]{0:T(128)}, u32[]{:S(2)}) copy-start(f32[128]{0:T(128)} %copy-done.17) | copy-start | bytes 1540
  758.8 2.6 copy-start.3
Sparse Core Ops, SparseCore 0:
  46.7 69.9 all-reduce.7
  360.4 63.0 all-reduce.9
  599.0 63.0 all-reduce.11
